TPU v7x, 32 devices: a whole 2x2x4 slice. The times are simulated.
32 devices in a mesh: clips: 2 (over y), tok: 4 (over z), head: 4 (over x, core).
Axes of the slice: x: 2, y: 2, z: 4, core: 2. Of those that a mesh axis runs over, the one named last changes fastest.
Arguments:
- query: bfloat16 [24, 256, 1536], P(('clips', 'tok'), 'head'), parts along dimension 0, may hold values from -16 to 16, as said below
- key: bfloat16 [24, 256, 1536], P(('clips', 'tok'), 'head'), parts along dimension 0, may hold values from -16 to 16
- value: bfloat16 [24, 256, 1536], P(('clips', 'tok'), 'head'), parts along dimension 0, may hold values from -6 to 6
- valid_rows: int32 [24], P(('clips', 'tok')), parts along dimension 0, may hold values from 1 to 8, as said below
Outputs:
- attended: bfloat16 [24, 256, 1536], P(('clips', 'tok'), 'head'), parts along dimension 0
There are 2 independent parts, one for each index of `clips`. A program takes and returns all parts, laid end to end along the dimension named above; each array names one. Nothing has to cross between parts.
Inputs may be any that keep to these rules, and one draw needn't show every extreme that they name: Entries of query and key lie within -16 and 16. `valid_rows`: tiles outside the last height-tile row have all 8 rows real; tiles of the last height-tile row each have their own count.
All inputs are finite; a program needn't handle non-finite values.
Results may differ from a plain program's by a relative error of at most 0.0031.
Values may be sent and summed in bfloat16 or wider, within the bound.
A program may use at most 64 MiB of HBM per device.

v0:
```python
import functools
import math

import jax
import jax.numpy as jnp
from jax import lax
from jax.experimental import pallas as pl
from jax.experimental.pallas import tpu as pltpu
from jax.sharding import PartitionSpec as P

HEAD_DIM = 128
TILE_H = 8
TILE_W = 8
TIME_TILES = 4
MESH = pl.DeviceIdType.MESH
GAIN = math.log2(math.e) / math.sqrt(HEAD_DIM)


def window_slots(rows_grid):
    sides = (-1, 0, 1) if rows_grid > 1 else (0,)
    around = [(down, side) for down in (-1, 0, 1) for side in sides if (down, side) != (0, 0)]
    return [(0, 0)] + around


def kernel(
    heads_axis, rows_grid,
    q_hbm, k_hbm, v_hbm, count_hbm, out_hbm,
    q_buf, k_buf, v_buf, bias_buf, s_buf, p_buf, inv_buf, acc_buf, o_buf, rows_buf, count_buf,
    local_sem, qx_send, qx_recv, kx_send, kx_recv, vx_send, vx_recv,
    bz_send, bz_recv, kz_send, kz_recv, vz_send, vz_recv, ox_send, ox_recv,
):
    slots = window_slots(rows_grid)
    width, part = q_hbm.shape[0], q_hbm.shape[1]
    tile_len, feats = q_buf.shape[1], q_buf.shape[2]
    local = feats // HEAD_DIM
    me = lax.axis_index("head")
    tok = lax.axis_index("tok")
    time, height = tok // rows_grid, tok % rows_grid
    steps = range(1, heads_axis)
    far_first = list(reversed(steps))

    def exists(j):
        down, side = slots[j]
        ok = (time + down >= 0) & (time + down < TIME_TILES)
        if side != 0:
            ok = ok & (height + side >= 0) & (height + side < rows_grid)
        return ok

    def around(j):
        return tok + slots[j][0] * rows_grid + slots[j][1]

    def opposite(j):
        return slots.index((-slots[j][0], -slots[j][1]))

    def peer(s):
        return me ^ s

    def rows(g):
        return pl.ds(pl.multiple_of(g * part, part), part)

    def cols(g):
        return pl.ds(pl.multiple_of(g * feats, feats), feats)

    def head_cols(h):
        return pl.ds(pl.multiple_of(h * HEAD_DIM, HEAD_DIM), HEAD_DIM)

    def global_cols(g, h):
        return pl.ds(pl.multiple_of((g * local + h) * HEAD_DIM, HEAD_DIM), HEAD_DIM)

    def remote(src, dst, send, recv, device):
        return pltpu.make_async_remote_copy(
            src_ref=src, dst_ref=dst, send_sem=send, recv_sem=recv,
            device_id=device, device_id_type=MESH,
        )

    def qx(s, owner):
        return remote(q_hbm.at[:, :, cols(peer(s))], q_buf.at[:, rows(owner), :],
                      qx_send.at[s], qx_recv.at[s], {"head": peer(s)})

    def kx(s, owner):
        return remote(k_hbm.at[:, :, cols(peer(s))], k_buf.at[0, :, rows(owner), :],
                      kx_send.at[s], kx_recv.at[s], {"head": peer(s)})

    def vx(h, n, s, owner):
        return remote(v_hbm.at[n, :, global_cols(peer(s), h)],
                      v_buf.at[0, n, rows(owner), head_cols(h)],
                      vx_send.at[h, n, s], vx_recv.at[h, n, s], {"head": peer(s)})

    def kz(j, s, slot):
        src = k_hbm.at[:, :, cols(me)] if s == 0 else k_buf.at[0, :, rows(peer(s)), :]
        return remote(src, k_buf.at[slot, :, rows(peer(s)), :],
                      kz_send.at[j, s], kz_recv.at[slot, s], {"tok": around(j)})

    def vz(j, h, n, s, slot):
        src = v_hbm.at[n, :, global_cols(me, h)] if s == 0 else v_buf.at[0, n, rows(peer(s)), head_cols(h)]
        return remote(src, v_buf.at[slot, n, rows(peer(s)), head_cols(h)],
                      vz_send.at[j, h, n, s], vz_recv.at[slot, h, n, s], {"tok": around(j)})

    def bz(j, slot):
        return remote(rows_buf.at[0], rows_buf.at[slot], bz_send.at[j], bz_recv.at[slot], {"tok": around(j)})

    def ox(h, c, s, owner):
        return remote(o_buf.at[c, rows(peer(s)), head_cols(h)],
                      out_hbm.at[c, :, global_cols(owner, h)],
                      ox_send.at[h, c, s], ox_recv.at[h, c, s], {"head": peer(s)})

    def each_neighbour(act):
        for j in range(1, len(slots)):
            pl.when(exists(j))(functools.partial(act, j))

    local_q = pltpu.make_async_copy(q_hbm.at[:, :, cols(me)], q_buf.at[:, rows(me), :], local_sem.at[0])
    local_k = pltpu.make_async_copy(k_hbm.at[:, :, cols(me)], k_buf.at[0, :, rows(me), :], local_sem.at[1])
    local_v = pltpu.make_async_copy(v_hbm.at[:, :, cols(me)], v_buf.at[0, :, rows(me), :], local_sem.at[2])
    local_c = pltpu.make_async_copy(count_hbm, count_buf, local_sem.at[3])

    barrier = pltpu.get_barrier_semaphore()
    for s in steps:
        pl.semaphore_signal(barrier, inc=1, device_id={"head": peer(s)}, device_id_type=MESH)
    partners = heads_axis - 1

    def greet(j):
        pl.semaphore_signal(barrier, inc=1, device_id={"tok": around(j)}, device_id_type=MESH)

    each_neighbour(greet)
    for j in range(1, len(slots)):
        partners = partners + jnp.where(exists(j), 1, 0)
    for copy in (local_c, local_q, local_k, local_v):
        copy.start()
    pl.semaphore_wait(barrier, partners)

    for s in far_first:
        kx(s, me).start()
    each_neighbour(lambda j: kz(j, 0, opposite(j)).start())
    for s in far_first:
        qx(s, me).start()
    for h in range(local):
        for n in range(width):
            for s in far_first:
                vx(h, n, s, me).start()

    local_c.wait()
    line = lax.broadcasted_iota(jnp.int32, rows_buf.shape[1:], 0)
    counts = jnp.zeros(rows_buf.shape[1:], jnp.int32)
    for n in range(width):
        counts = jnp.where(line == n, count_buf[n], counts)
    rows_buf[0] = counts

    for j in range(1, len(slots)):
        @pl.when(jnp.logical_not(exists(j)))
        def _(j=j):
            k_buf[j] = jnp.zeros(k_buf.shape[1:], k_buf.dtype)
            v_buf[j] = jnp.zeros(v_buf.shape[1:], v_buf.dtype)
            rows_buf[j] = jnp.zeros(rows_buf.shape[1:], rows_buf.dtype)

    order = [1] + [s for s in far_first if s != 1] if heads_axis > 1 else []
    for s in order:
        kx(s, peer(s)).wait_recv()
        each_neighbour(lambda j, s=s: kz(j, s, opposite(j)).start())
    near = [s for s in steps if s == 1]
    later = [s for s in order if s != 1]
    each_neighbour(lambda j: bz(j, opposite(j)).start())

    def values_on(h, n, s):
        if s != 0:
            vx(h, n, s, peer(s)).wait_recv()
        each_neighbour(lambda j: vz(j, h, n, s, opposite(j)).start())

    for h in range(local):
        for n in range(width):
            for s in [0] + near:
                values_on(h, n, s)

    for copy in (local_q, local_k, local_v):
        copy.wait()
    for s in steps:
        qx(s, peer(s)).wait_recv()

    def keys_in(j):
        bz(j, j).wait_recv()
        for s in range(heads_axis):
            kz(j, s, j).wait_recv()

    each_neighbour(keys_in)

    row = lax.broadcasted_iota(jnp.int32, bias_buf.shape[2:], 1) // TILE_W % TILE_H
    for j in range(len(slots)):
        for n in range(width):
            real = jnp.broadcast_to(rows_buf[j, n:n + 1, 0:1], row.shape)
            bias_buf[j, n] = jnp.where(row < real, 0.0, -jnp.inf)

    def window(c):
        return [(j, n) for j in range(len(slots)) for n in range(width) if abs(n - c) <= 1]

    def weigh(h, carry):
        for c in range(width):
            scratch = s_buf.at[c % s_buf.shape[0]]
            q = q_buf[c, :, head_cols(h)]
            top = None
            for i, (j, n) in enumerate(window(c)):
                s = lax.dot_general(q, k_buf[j, n, :, head_cols(h)], (((1,), (1,)), ((), ())),
                                    preferred_element_type=jnp.float32)
                s = s + bias_buf[j, n, 0:1, :]
                scratch[:, i * tile_len:(i + 1) * tile_len] = s
                for half in range(0, tile_len, 128):
                    piece = s[:, half:half + 128]
                    top = piece if top is None else jnp.maximum(top, piece)
            largest = jnp.max(top, axis=-1, keepdims=True)
            total = None
            for i in range(len(window(c))):
                for half in range(0, tile_len, 128):
                    at = slice(i * tile_len + half, i * tile_len + half + 128)
                    weight = jnp.exp2((scratch[:, at] - largest) * GAIN)
                    total = weight if total is None else total + weight
                    p_buf[h, c, :, at] = weight.astype(jnp.bfloat16)
            inverse = 1.0 / jnp.sum(total, axis=-1, keepdims=True)
            inv_buf[h, c] = jnp.broadcast_to(inverse, (tile_len, HEAD_DIM))
        for n in range(width):
            for s in later:
                values_on(h, n, s)
        return carry

    lax.fori_loop(0, local, weigh, 0)

    def local_out(h, c):
        return pltpu.make_async_copy(o_buf.at[c, rows(me), head_cols(h)],
                                     out_hbm.at[c, :, global_cols(me, h)], local_sem.at[4 + h * width + c])

    if heads_axis % 2 == 0:
        half = heads_axis // 2
        span = tile_len // 2
        side = me // half
        blocks = [
            (pl.ds(pl.multiple_of((1 - side) * span, span), span), [s for s in far_first if s >= half]),
            (pl.ds(pl.multiple_of(side * span, span), span), [s for s in far_first if s < half]),
        ]
    else:
        blocks = [(slice(None), far_first)]

    def mix(h, carry):
        def gather(c, at, picked):
            summed = None
            for i, (j, n) in enumerate(window(c)):
                if picked(j, n):
                    term = jnp.dot(p_buf[h, c, at, i * tile_len:(i + 1) * tile_len],
                                   v_buf[j, n, :, head_cols(h)], preferred_element_type=jnp.float32)
                    summed = term if summed is None else summed + term
            return summed

        for c in range(width):
            acc_buf[c] = gather(c, slice(None), lambda j, n: j == 0)
        for n in range(width):
            def values_in(j, n=n):
                for s in range(heads_axis):
                    vz(j, h, n, s, j).wait_recv()

            each_neighbour(values_in)
            here = [c for c in range(width) if abs(n - c) <= 1]
            done = [c for c in here if n == min(c + 1, width - 1)]
            for at, partners_at in blocks:
                for c in done:
                    summed = acc_buf[c, at] + gather(c, at, lambda j, m: j != 0 and m == n)
                    o_buf[c, at, head_cols(h)] = (summed * inv_buf[h, c, at]).astype(o_buf.dtype)
                    for s in partners_at:
                        ox(h, c, s, me).start()
            for c in done:
                local_out(h, c).start()
            for c in here:
                if c not in done:
                    acc_buf[c] = acc_buf[c] + gather(c, slice(None), lambda j, m: j != 0 and m == n)
        return carry

    lax.fori_loop(0, local, mix, 0)

    for s in steps:
        kx(s, me).wait_send()
        qx(s, me).wait_send()
        for h in range(local):
            for n in range(width):
                vx(h, n, s, me).wait_send()

    def sent(j):
        bz(j, opposite(j)).wait_send()
        for s in range(heads_axis):
            kz(j, s, opposite(j)).wait_send()
            for h in range(local):
                for n in range(width):
                    vz(j, h, n, s, opposite(j)).wait_send()

    each_neighbour(sent)
    for h in range(local):
        for c in range(width):
            local_out(h, c).wait()
            for s in steps:
                ox(h, c, s, me).wait_send()
                ox(h, c, s, peer(s)).wait_recv()


def body(heads_axis, tok_axis, query, key, value, valid_rows):
    width, part, wide = query.shape
    rows_grid = tok_axis // TIME_TILES
    tile_len, feats = part * heads_axis, wide // heads_axis
    local = feats // HEAD_DIM
    slots = len(window_slots(rows_grid))
    most = slots * min(width, 3) * tile_len
    dma = pltpu.SemaphoreType.DMA
    any_space = pl.BlockSpec(memory_space=pl.ANY)
    return pl.pallas_call(
        functools.partial(kernel, heads_axis, rows_grid),
        out_shape=jax.ShapeDtypeStruct(query.shape, query.dtype),
        in_specs=[pl.BlockSpec(memory_space=pltpu.HBM)] * 4,
        out_specs=any_space,
        scratch_shapes=[
            pltpu.VMEM((width, tile_len, feats), jnp.bfloat16),
            pltpu.VMEM((slots, width, tile_len, feats), jnp.bfloat16),
            pltpu.VMEM((slots, width, tile_len, feats), jnp.bfloat16),
            pltpu.VMEM((slots, width, 8, tile_len), jnp.float32),
            pltpu.VMEM((3 if slots <= 3 else 1, tile_len, most), jnp.float32),
            pltpu.VMEM((local, width, tile_len, most), jnp.bfloat16),
            pltpu.VMEM((local, width, tile_len, HEAD_DIM), jnp.float32),
            pltpu.VMEM((width, tile_len, HEAD_DIM), jnp.float32),
            pltpu.VMEM((width, tile_len, feats), jnp.bfloat16),
            pltpu.VMEM((slots, -(-width // 8) * 8, 128), jnp.int32),
            pltpu.SMEM((width,), jnp.int32),
            dma((4 + local * width,)),
            dma((heads_axis,)), dma((heads_axis,)),
            dma((heads_axis,)), dma((heads_axis,)),
            dma((local, width, heads_axis)), dma((local, width, heads_axis)),
            dma((slots,)), dma((slots,)),
            dma((slots, heads_axis)), dma((slots, heads_axis)),
            dma((slots, local, width, heads_axis)), dma((slots, local, width, heads_axis)),
            dma((local, width, heads_axis)), dma((local, width, heads_axis)),
        ],
        compiler_params=pltpu.CompilerParams(
            collective_id=0, has_side_effects=True, vmem_limit_bytes=36_000_000 if slots <= 3 else 63_000_000
        ),
    )(*(pltpu.with_memory_space_constraint(x, pltpu.HBM) for x in (query, key, value, valid_rows)))


def solution(mesh):
    placed = (
        P(("clips", "tok"), "head", None),
        P(("clips", "tok"), "head", None),
        P(("clips", "tok"), "head", None),
        P(("clips", "tok")),
    )
    return jax.shard_map(
        functools.partial(body, mesh.shape["head"], mesh.shape["tok"]),
        mesh=mesh,
        in_specs=placed,
        out_specs=P(("clips", "tok"), "head", None),
        check_vma=False,
    )
```

profile of v0, /device:TPU:0, one launch (start us, length us, event | category | flops | bytes accessed | tf_op | source)
XLA Modules:
  0.0 39.7 jit_solution(15981096140792327244)
XLA Ops:
  0.0 38.9 %shard_map.46 = bf16[3,64,1536]{2,1,0:T(8,128)(2,1)S(1)} custom-call(bf16[3,64,1536]{2,1,0:T(8,128)(2,1)} %q_hbm.1, bf16[3,64,1536]{2,1,0:T(8,128)(2,1)} %k_hbm.1, bf16[3,64,1536]{2,1,0:T(8,128)(2,1)} %v_hbm.1, s32[3]{0:T(128)} %count_hbm.1), custom_call_target="tpu_custom_call" | custom-call | tf_op jit(solution)/shard_map/pallas_call | solution.py:307
  38.9 0.8 %copy.6 = bf16[3,64,1536]{2,1,0:T(8,128)(2,1)} copy(bf16[3,64,1536]{2,1,0:T(8,128)(2,1)S(1)} %shard_map.46) | data formatting | bytes 1179648
where the time goes:
time: 39.8 us; the launch traced here: 39.7 us
  Pallas kernels  38.9 us (98%)
  local copies, waits for them, and re-layouts  0.82 us (2%)
    pallas_call x1, Pallas kernels, body(): pl.pallas_call(functools.partial(kernel, heads_axis, rows_grid), out_shap...  38.9 us
    unnamed x1, local copies, waits for them, and re-layouts  0.82 us

commit v1 on v0

--- a/solution.py
+++ b/solution.py
@@ -336,6 +336,362 @@
     )(*(pltpu.with_memory_space_constraint(x, pltpu.HBM) for x in (query, key, value, valid_rows)))
 
 
+def by_head(
+    q_hbm, k_hbm, v_hbm, count_hbm, out_hbm,
+    q_buf, k_buf, v_buf, bias_buf, s_buf, p_buf, inv_buf, acc_buf, o_buf, rows_buf, count_buf,
+    lq_sem, lk_sem, lv_sem, lc_sem, lo_sem, qx_send, qx_recv, kx_send, kx_recv, vx_send, vx_recv,
+    bz_send, bz_recv, kz_send, kz_recv, vz_send, vz_recv, ox_send, ox_recv,
+):
+    local, width, tile_len = q_buf.shape[0], q_buf.shape[1], q_buf.shape[2]
+    part = q_hbm.shape[1]
+    me = lax.axis_index("head")
+    tok = lax.axis_index("tok")
+    side = me // 2
+    half = tile_len // 2
+    far, last = (3, 2), local - 1
+    slots = (0, -1, 1)
+    opposite = (0, 2, 1)
+
+    def exists(j):
+        return (tok + slots[j] >= 0) & (tok + slots[j] < TIME_TILES)
+
+    def peer(s):
+        return me ^ s
+
+    def rows(g):
+        return pl.ds(pl.multiple_of(g * part, part), part)
+
+    def cols(g, h):
+        return pl.ds(pl.multiple_of((g * local + h) * HEAD_DIM, HEAD_DIM), HEAD_DIM)
+
+    def remote(src, dst, send, recv, device):
+        return pltpu.make_async_remote_copy(
+            src_ref=src, dst_ref=dst, send_sem=send, recv_sem=recv,
+            device_id=device, device_id_type=MESH,
+        )
+
+    def spread(hbm, buf, send, recv):
+        def copy(h, s, owner):
+            return remote(hbm.at[:, :, cols(peer(s), h)], buf(h).at[:, rows(owner), :],
+                          send.at[h, s], recv.at[h, s], {"head": peer(s)})
+        return copy
+
+    qx = spread(q_hbm, lambda h: q_buf.at[h], qx_send, qx_recv)
+    kx = spread(k_hbm, lambda h: k_buf.at[0, h], kx_send, kx_recv)
+    vx = spread(v_hbm, lambda h: v_buf.at[0, h], vx_send, vx_recv)
+
+    def along(buf, send, recv):
+        def copy(j, h, s, slot, n=None):
+            pick = slice(None) if n is None else slice(n, n + 1)
+            at = 0 if n is None else n
+            return remote(buf.at[0, h, pick, rows(peer(s)), :], buf.at[slot, h, pick, rows(peer(s)), :],
+                          send.at[j, h, s, at], recv.at[slot, h, s, at], {"tok": tok + slots[j]})
+        return copy
+
+    kz = along(k_buf, kz_send, kz_recv)
+    vz = along(v_buf, vz_send, vz_recv)
+
+    def vz_tiles(h, s):
+        return tuple(range(width)) if h == last and s in far else (None,)
+
+    def bz(j, slot):
+        return remote(rows_buf.at[0], rows_buf.at[slot], bz_send.at[j], bz_recv.at[slot], {"tok": tok + slots[j]})
+
+    def ox(h, c, s, owner):
+        return remote(o_buf.at[h, c, rows(peer(s)), :], out_hbm.at[c, :, cols(owner, h)],
+                      ox_send.at[h, c, s], ox_recv.at[h, c, s], {"head": peer(s)})
+
+    def own(hbm, buf, sem):
+        return [pltpu.make_async_copy(hbm.at[:, :, cols(me, h)], buf(h).at[:, rows(me), :], sem.at[h])
+                for h in range(local)]
+
+    own_k = own(k_hbm, lambda h: k_buf.at[0, h], lk_sem)
+    own_v = own(v_hbm, lambda h: v_buf.at[0, h], lv_sem)
+    own_q = own(q_hbm, lambda h: q_buf.at[h], lq_sem)
+    own_c = pltpu.make_async_copy(count_hbm, count_buf, lc_sem)
+
+    def own_o(h, c):
+        return pltpu.make_async_copy(o_buf.at[h, c, rows(me), :], out_hbm.at[c, :, cols(me, h)], lo_sem.at[h, c])
+
+    def each_neighbour(act):
+        for j in (1, 2):
+            pl.when(exists(j))(functools.partial(act, j))
+
+    barrier = pltpu.get_barrier_semaphore()
+
+    def greet(j):
+        pl.semaphore_signal(barrier, inc=1, device_id={"tok": tok + slots[j]}, device_id_type=MESH)
+
+    each_neighbour(greet)
+    for s in (2, 3, 1):
+        pl.semaphore_signal(barrier, inc=1, device_id={"head": peer(s)}, device_id_type=MESH)
+    own_c.start()
+    for h in range(local):
+        own_k[h].start()
+        own_v[h].start()
+    for h in range(local):
+        own_q[h].start()
+    for j in (1, 2):
+        @pl.when(jnp.logical_not(exists(j)))
+        def _(j=j):
+            k_buf[j] = jnp.zeros(k_buf.shape[1:], k_buf.dtype)
+            v_buf[j] = jnp.zeros(v_buf.shape[1:], v_buf.dtype)
+            rows_buf[j] = jnp.zeros(rows_buf.shape[1:], rows_buf.dtype)
+    own_c.wait()
+    line = lax.broadcasted_iota(jnp.int32, rows_buf.shape[1:], 0)
+    counts = jnp.zeros(rows_buf.shape[1:], jnp.int32)
+    for n in range(width):
+        counts = jnp.where(line == n, count_buf[n], counts)
+    rows_buf[0] = counts
+    for h in range(local):
+        own_k[h].wait()
+        own_v[h].wait()
+    pl.semaphore_wait(barrier, 3 + jnp.where(exists(1), 1, 0) + jnp.where(exists(2), 1, 0))
+
+    def across(copy, h):
+        for s in far:
+            copy(h, s, me).start()
+
+    def beside(copy, h):
+        copy(h, 1, me).start()
+
+    def onward(copy, h, s, tiles=(None,)):
+        def act(j):
+            for n in tiles:
+                copy(j, h, s, opposite[j], n).start()
+        each_neighbour(act)
+
+    def onward_v(h, s):
+        onward(vz, h, s, vz_tiles(h, s))
+
+    across(kx, 0)
+    onward(kz, 0, 0)
+    beside(kx, 0)
+    across(vx, 0)
+    onward_v(0, 0)
+    beside(vx, 0)
+    across(qx, 0)
+    for h in range(1, local):
+        beside(kx, h)
+        beside(vx, h)
+    across(kx, 1)
+    onward(kz, 1, 0)
+    across(vx, 1)
+    onward_v(1, 0)
+    across(kx, 2)
+    across(qx, 1)
+    across(vx, 2)
+    across(qx, 2)
+    each_neighbour(lambda j: bz(j, opposite[j]).start())
+    for h in range(local):
+        beside(qx, h)
+
+    for h in (0, 1):
+        kx(h, 1, peer(1)).wait_recv()
+        onward(kz, h, 1)
+        vx(h, 1, peer(1)).wait_recv()
+        onward_v(h, 1)
+    for s in far:
+        kx(0, s, peer(s)).wait_recv()
+        onward(kz, 0, s)
+    for s in far:
+        vx(0, s, peer(s)).wait_recv()
+        onward_v(0, s)
+    onward(kz, last, 0)
+    kx(last, 1, peer(1)).wait_recv()
+    onward(kz, last, 1)
+    vx(last, 1, peer(1)).wait_recv()
+
+    each_neighbour(lambda j: bz(j, j).wait_recv())
+    row = lax.broadcasted_iota(jnp.int32, bias_buf.shape[2:], 1) // TILE_W % TILE_H
+    for j in range(3):
+        for n in range(width):
+            real = jnp.broadcast_to(rows_buf[j, n:n + 1, 0:1], row.shape)
+            bias_buf[j, n] = jnp.where(row < real, 0.0, -jnp.inf)
+
+    for s in far:
+        kx(1, s, peer(s)).wait_recv()
+        onward(kz, 1, s)
+    for s in far:
+        vx(1, s, peer(s)).wait_recv()
+        onward_v(1, s)
+
+    def window(c):
+        return [(j, n) for j in range(3) for n in range(width) if abs(n - c) <= 1]
+
+    def queries_in(h):
+        own_q[h].wait()
+        for s in (1, 2, 3):
+            qx(h, s, peer(s)).wait_recv()
+
+    def keys_in(h):
+        def act(j):
+            for s in range(4):
+                kz(j, h, s, j).wait_recv()
+        each_neighbour(act)
+
+    def values_in(h, which, tiles=None):
+        def act(j):
+            for s in which:
+                for n in (tiles if tiles is not None else vz_tiles(h, s)):
+                    vz(j, h, s, j, n).wait_recv()
+        each_neighbour(act)
+
+    def weigh(h):
+        for c in range(width):
+            scratch = s_buf.at[c]
+            q = q_buf[h, c]
+            top = None
+            for i, (j, n) in enumerate(window(c)):
+                s = lax.dot_general(q, k_buf[j, h, n], (((1,), (1,)), ((), ())),
+                                    preferred_element_type=jnp.float32)
+                s = s + bias_buf[j, n, 0:1, :]
+                scratch[:, i * tile_len:(i + 1) * tile_len] = s
+                for at in range(0, tile_len, 128):
+                    piece = s[:, at:at + 128]
+                    top = piece if top is None else jnp.maximum(top, piece)
+            largest = jnp.max(top, axis=-1, keepdims=True)
+            total = None
+            for i in range(len(window(c))):
+                for at in range(0, tile_len, 128):
+                    at = slice(i * tile_len + at, i * tile_len + at + 128)
+                    weight = jnp.exp2((scratch[:, at] - largest) * GAIN)
+                    total = weight if total is None else total + weight
+                    p_buf[c, :, at] = weight.astype(jnp.bfloat16)
+            inverse = 1.0 / jnp.sum(total, axis=-1, keepdims=True)
+            inv_buf[c] = jnp.broadcast_to(inverse, (tile_len, HEAD_DIM))
+
+    there = pl.ds(pl.multiple_of((1 - side) * half, half), half)
+    here = pl.ds(pl.multiple_of(side * half, half), half)
+    blocks = ((there, far), (here, (1,)))
+
+    def mixed(h, c, at, picked, keys=None):
+        summed = None
+        for i, (j, n) in enumerate(window(c)):
+            if picked(j, n):
+                if keys is None:
+                    p, v = p_buf[c, at, i * tile_len:(i + 1) * tile_len], v_buf[j, h, n]
+                else:
+                    span = pl.ds(pl.multiple_of(i * tile_len + keys * half, half), half)
+                    p, v = p_buf[c, at, span], v_buf[j, h, n, pl.ds(pl.multiple_of(keys * half, half), half), :]
+                term = jnp.dot(p, v, preferred_element_type=jnp.float32)
+                summed = term if summed is None else summed + term
+        return summed
+
+    def leave(h, c, at, partners, summed):
+        o_buf[h, c, at, :] = (summed * inv_buf[c, at]).astype(o_buf.dtype)
+        for s in partners:
+            ox(h, c, s, me).start()
+
+    def mix(h):
+        for c in range(width):
+            for at, partners in blocks:
+                leave(h, c, at, partners, mixed(h, c, at, lambda j, n: True))
+            own_o(h, c).start()
+
+    def mix_last(h):
+        for c in range(width):
+            acc_buf[c] = mixed(h, c, slice(None), lambda j, n: j == 0)
+        values_in(h, (0, 1))
+        for c in range(width):
+            acc_buf[c] = acc_buf[c] + mixed(h, c, slice(None), lambda j, n: j != 0, side)
+        for n in range(width):
+            values_in(h, far, (n,))
+            near = [c for c in range(width) if abs(n - c) <= 1]
+            done = [c for c in near if n == min(c + 1, width - 1)]
+            for at, partners in blocks:
+                for c in done:
+                    leave(h, c, at, partners,
+                          acc_buf[c, at] + mixed(h, c, at, lambda j, m: j != 0 and m == n, 1 - side))
+            for c in done:
+                own_o(h, c).start()
+            for c in near:
+                if c not in done:
+                    acc_buf[c] = acc_buf[c] + mixed(h, c, slice(None), lambda j, m: j != 0 and m == n, 1 - side)
+
+    queries_in(0)
+    keys_in(0)
+    weigh(0)
+    for s in far:
+        kx(last, s, peer(s)).wait_recv()
+        onward(kz, last, s)
+    onward_v(last, 0)
+    onward_v(last, 1)
+    values_in(0, range(4))
+    mix(0)
+    for s in far:
+        vx(last, s, peer(s)).wait_recv()
+    for n in range(width):
+        for s in far:
+            onward(vz, last, s, (n,))
+    queries_in(1)
+    keys_in(1)
+    weigh(1)
+    values_in(1, range(4))
+    mix(1)
+    queries_in(last)
+    keys_in(last)
+    weigh(last)
+    mix_last(last)
+
+    for h in range(local):
+        for s in (1, 2, 3):
+            kx(h, s, me).wait_send()
+            vx(h, s, me).wait_send()
+            qx(h, s, me).wait_send()
+
+    def sent(j):
+        bz(j, opposite[j]).wait_send()
+        for h in range(local):
+            for s in range(4):
+                kz(j, h, s, opposite[j]).wait_send()
+                for n in vz_tiles(h, s):
+                    vz(j, h, s, opposite[j], n).wait_send()
+
+    each_neighbour(sent)
+    for h in range(local):
+        for c in range(width):
+            own_o(h, c).wait()
+            for s in (1, 2, 3):
+                ox(h, c, s, me).wait_send()
+                ox(h, c, s, peer(s)).wait_recv()
+
+
+def body_by_head(query, key, value, valid_rows):
+    width, part, wide = query.shape
+    tile_len, local = part * 4, wide // 4 // HEAD_DIM
+    most = 3 * min(width, 3) * tile_len
+    dma = pltpu.SemaphoreType.DMA
+    return pl.pallas_call(
+        by_head,
+        out_shape=jax.ShapeDtypeStruct(query.shape, query.dtype),
+        in_specs=[pl.BlockSpec(memory_space=pltpu.HBM)] * 4,
+        out_specs=pl.BlockSpec(memory_space=pl.ANY),
+        scratch_shapes=[
+            pltpu.VMEM((local, width, tile_len, HEAD_DIM), jnp.bfloat16),
+            pltpu.VMEM((3, local, width, tile_len, HEAD_DIM), jnp.bfloat16),
+            pltpu.VMEM((3, local, width, tile_len, HEAD_DIM), jnp.bfloat16),
+            pltpu.VMEM((3, width, 8, tile_len), jnp.float32),
+            pltpu.VMEM((width, tile_len, most), jnp.float32),
+            pltpu.VMEM((width, tile_len, most), jnp.bfloat16),
+            pltpu.VMEM((width, tile_len, HEAD_DIM), jnp.float32),
+            pltpu.VMEM((width, tile_len, HEAD_DIM), jnp.float32),
+            pltpu.VMEM((local, width, tile_len, HEAD_DIM), jnp.bfloat16),
+            pltpu.VMEM((3, -(-width // 8) * 8, 128), jnp.int32),
+            pltpu.SMEM((width,), jnp.int32),
+            dma((local,)), dma((local,)), dma((local,)), dma(()), dma((local, width)),
+            dma((local, 4)), dma((local, 4)), dma((local, 4)), dma((local, 4)), dma((local, 4)), dma((local, 4)),
+            dma((3,)), dma((3,)),
+            dma((3, local, 4, 1)), dma((3, local, 4, 1)),
+            dma((3, local, 4, width)), dma((3, local, 4, width)),
+            dma((local, width, 4)), dma((local, width, 4)),
+        ],
+        compiler_params=pltpu.CompilerParams(
+            collective_id=0, has_side_effects=True, vmem_limit_bytes=36_000_000
+        ),
+    )(*(pltpu.with_memory_space_constraint(x, pltpu.HBM) for x in (query, key, value, valid_rows)))
+
+
 def solution(mesh):
     placed = (
         P(("clips", "tok"), "head", None),
@@ -343,8 +699,15 @@
         P(("clips", "tok"), "head", None),
         P(("clips", "tok")),
     )
+    heads_axis, tok_axis = mesh.shape["head"], mesh.shape["tok"]
+
+    def step(query, key, value, valid_rows):
+        if heads_axis == 4 and tok_axis == TIME_TILES and query.shape[2] == 4 * 3 * HEAD_DIM:
+            return body_by_head(query, key, value, valid_rows)
+        return body(heads_axis, tok_axis, query, key, value, valid_rows)
+
     return jax.shard_map(
-        functools.partial(body, mesh.shape["head"], mesh.shape["tok"]),
+        step,
         mesh=mesh,
         in_specs=placed,
         out_specs=P(("clips", "tok"), "head", None),

time: 39.8 us -> 39.6 us (level)
  no operation moved by 1% of the time
where the time goes in v1:
time: 39.6 us; the launch traced here: 39.4 us
  Pallas kernels  38.6 us (97%)
  local copies, waits for them, and re-layouts  0.82 us (2%)
    pallas_call x1, Pallas kernels, body_by_head(): pl.pallas_call(by_head, out_shape=jax.ShapeDtypeStruct(query.shape, query...  38.6 us
    unnamed x1, local copies, waits for them, and re-layouts  0.82 us

profile of v1, /device:TPU:0, one launch (start us, length us, event | category | flops | bytes accessed | tf_op | source)
XLA Modules:
  0.0 39.4 jit_solution(15649118301031196928)
XLA Ops:
  0.0 38.6 %shard_map.46 = bf16[3,64,1536]{2,1,0:T(8,128)(2,1)S(1)} custom-call(bf16[3,64,1536]{2,1,0:T(8,128)(2,1)} %q_hbm.1, bf16[3,64,1536]{2,1,0:T(8,128)(2,1)} %k_hbm.1, bf16[3,64,1536]{2,1,0:T(8,128)(2,1)} %v_hbm.1, s32[3]{0:T(128)} %count_hbm.1), custom_call_target="tpu_custom_call" | custom-call | tf_op jit(solution)/shard_map/pallas_call | solution.py:665
  38.6 0.8 %copy.6 = bf16[3,64,1536]{2,1,0:T(8,128)(2,1)} copy(bf16[3,64,1536]{2,1,0:T(8,128)(2,1)S(1)} %shard_map.46) | data formatting | bytes 1179648

commit v2 on v1

--- a/solution.py
+++ b/solution.py
@@ -373,33 +373,34 @@
     def spread(hbm, buf, send, recv):
         def copy(h, s, owner):
             return remote(hbm.at[:, :, cols(peer(s), h)], buf(h).at[:, rows(owner), :],
-                          send.at[h, s], recv.at[h, s], {"head": peer(s)})
+                          send.at[h, s - 1], recv.at[h, s - 1], {"head": peer(s)})
         return copy
 
     qx = spread(q_hbm, lambda h: q_buf.at[h], qx_send, qx_recv)
     kx = spread(k_hbm, lambda h: k_buf.at[0, h], kx_send, kx_recv)
     vx = spread(v_hbm, lambda h: v_buf.at[0, h], vx_send, vx_recv)
 
-    def along(buf, send, recv):
+    def along(hbm, buf, send, recv):
         def copy(j, h, s, slot, n=None):
             pick = slice(None) if n is None else slice(n, n + 1)
-            at = 0 if n is None else n
-            return remote(buf.at[0, h, pick, rows(peer(s)), :], buf.at[slot, h, pick, rows(peer(s)), :],
-                          send.at[j, h, s, at], recv.at[slot, h, s, at], {"tok": tok + slots[j]})
+            at = h * 4 + s if not n else local * 4 + (s - 2) * (width - 1) + n - 1
+            src = hbm.at[pick, :, cols(me, h)] if s == 0 else buf.at[0, h, pick, rows(peer(s)), :]
+            return remote(src, buf.at[slot, h, pick, rows(peer(s)), :],
+                          send.at[j - 1, at], recv.at[slot - 1, at], {"tok": tok + slots[j]})
         return copy
 
-    kz = along(k_buf, kz_send, kz_recv)
-    vz = along(v_buf, vz_send, vz_recv)
+    kz = along(k_hbm, k_buf, kz_send, kz_recv)
+    vz = along(v_hbm, v_buf, vz_send, vz_recv)
 
     def vz_tiles(h, s):
         return tuple(range(width)) if h == last and s in far else (None,)
 
     def bz(j, slot):
-        return remote(rows_buf.at[0], rows_buf.at[slot], bz_send.at[j], bz_recv.at[slot], {"tok": tok + slots[j]})
+        return remote(rows_buf.at[0], rows_buf.at[slot], bz_send.at[j - 1], bz_recv.at[slot - 1], {"tok": tok + slots[j]})
 
     def ox(h, c, s, owner):
         return remote(o_buf.at[h, c, rows(peer(s)), :], out_hbm.at[c, :, cols(owner, h)],
-                      ox_send.at[h, c, s], ox_recv.at[h, c, s], {"head": peer(s)})
+                      ox_send.at[h, c, s - 1], ox_recv.at[h, c, s - 1], {"head": peer(s)})
 
     def own(hbm, buf, sem):
         return [pltpu.make_async_copy(hbm.at[:, :, cols(me, h)], buf(h).at[:, rows(me), :], sem.at[h])
@@ -431,21 +432,6 @@
         own_v[h].start()
     for h in range(local):
         own_q[h].start()
-    for j in (1, 2):
-        @pl.when(jnp.logical_not(exists(j)))
-        def _(j=j):
-            k_buf[j] = jnp.zeros(k_buf.shape[1:], k_buf.dtype)
-            v_buf[j] = jnp.zeros(v_buf.shape[1:], v_buf.dtype)
-            rows_buf[j] = jnp.zeros(rows_buf.shape[1:], rows_buf.dtype)
-    own_c.wait()
-    line = lax.broadcasted_iota(jnp.int32, rows_buf.shape[1:], 0)
-    counts = jnp.zeros(rows_buf.shape[1:], jnp.int32)
-    for n in range(width):
-        counts = jnp.where(line == n, count_buf[n], counts)
-    rows_buf[0] = counts
-    for h in range(local):
-        own_k[h].wait()
-        own_v[h].wait()
     pl.semaphore_wait(barrier, 3 + jnp.where(exists(1), 1, 0) + jnp.where(exists(2), 1, 0))
 
     def across(copy, h):
@@ -482,7 +468,6 @@
     across(qx, 1)
     across(vx, 2)
     across(qx, 2)
-    each_neighbour(lambda j: bz(j, opposite[j]).start())
     for h in range(local):
         beside(qx, h)
 
@@ -491,6 +476,22 @@
         onward(kz, h, 1)
         vx(h, 1, peer(1)).wait_recv()
         onward_v(h, 1)
+    for j in (1, 2):
+        @pl.when(jnp.logical_not(exists(j)))
+        def _(j=j):
+            k_buf[j] = jnp.zeros(k_buf.shape[1:], k_buf.dtype)
+            v_buf[j] = jnp.zeros(v_buf.shape[1:], v_buf.dtype)
+            rows_buf[j] = jnp.zeros(rows_buf.shape[1:], rows_buf.dtype)
+    own_c.wait()
+    line = lax.broadcasted_iota(jnp.int32, rows_buf.shape[1:], 0)
+    counts = jnp.zeros(rows_buf.shape[1:], jnp.int32)
+    for n in range(width):
+        counts = jnp.where(line == n, count_buf[n], counts)
+    rows_buf[0] = counts
+    each_neighbour(lambda j: bz(j, opposite[j]).start())
+    for h in range(local):
+        own_k[h].wait()
+        own_v[h].wait()
     for s in far:
         kx(0, s, peer(s)).wait_recv()
         onward(kz, 0, s)
@@ -680,11 +681,11 @@
             pltpu.VMEM((3, -(-width // 8) * 8, 128), jnp.int32),
             pltpu.SMEM((width,), jnp.int32),
             dma((local,)), dma((local,)), dma((local,)), dma(()), dma((local, width)),
-            dma((local, 4)), dma((local, 4)), dma((local, 4)), dma((local, 4)), dma((local, 4)), dma((local, 4)),
-            dma((3,)), dma((3,)),
-            dma((3, local, 4, 1)), dma((3, local, 4, 1)),
-            dma((3, local, 4, width)), dma((3, local, 4, width)),
-            dma((local, width, 4)), dma((local, width, 4)),
+            dma((local, 3)), dma((local, 3)), dma((local, 3)), dma((local, 3)), dma((local, 3)), dma((local, 3)),
+            dma((2,)), dma((2,)),
+            dma((2, local * 4)), dma((2, local * 4)),
+            dma((2, local * 4 + 2 * (width - 1))), dma((2, local * 4 + 2 * (width - 1))),
+            dma((local, width, 3)), dma((local, width, 3)),
         ],
         compiler_params=pltpu.CompilerParams(
             collective_id=0, has_side_effects=True, vmem_limit_bytes=36_000_000

time: 39.6 us -> 37.9 us (0.957)
  Pallas kernels: 38.6 us -> 36.9 us
    pallas_call x1, Pallas kernels: 38.6 us -> 36.9 us  [body_by_head(): pl.pallas_call(by_head, out_shape=jax.ShapeDtypeStruct(query.shape, query...]
where the time goes in v2:
time: 37.9 us; the launch traced here: 37.7 us
  Pallas kernels  36.9 us (97%)
  local copies, waits for them, and re-layouts  0.82 us (2%)
    pallas_call x1, Pallas kernels, body_by_head(): pl.pallas_call(by_head, out_shape=jax.ShapeDtypeStruct(query.shape, query...  36.9 us
    unnamed x1, local copies, waits for them, and re-layouts  0.82 us

profile of v2, /device:TPU:0, one launch (start us, length us, event | category | flops | bytes accessed | tf_op | source)
XLA Modules:
  0.0 37.7 jit_solution(8622948906674705873)
XLA Ops:
  0.0 36.9 %shard_map.46 = bf16[3,64,1536]{2,1,0:T(8,128)(2,1)S(1)} custom-call(bf16[3,64,1536]{2,1,0:T(8,128)(2,1)} %q_hbm.1, bf16[3,64,1536]{2,1,0:T(8,128)(2,1)} %k_hbm.1, bf16[3,64,1536]{2,1,0:T(8,128)(2,1)} %v_hbm.1, s32[3]{0:T(128)} %count_hbm.1), custom_call_target="tpu_custom_call" | custom-call | tf_op jit(solution)/shard_map/pallas_call | solution.py:666
  36.9 0.8 %copy.6 = bf16[3,64,1536]{2,1,0:T(8,128)(2,1)} copy(bf16[3,64,1536]{2,1,0:T(8,128)(2,1)S(1)} %shard_map.46) | data formatting | bytes 1179648
